TPU v7x, 32 devices: a whole 2x2x4 slice. The times are simulated.
32 devices in a mesh: groups: 2 (over y), item: 4 (over z), dp: 2 (over core), tensor: 2 (over x).
Axes of the slice: x: 2, y: 2, z: 4, core: 2. Of those that a mesh axis runs over, the one named last changes fastest.
Arguments:
- events: bfloat16 [12288, 1024], P(('groups', 'item', 'dp')), parts along dimension 0, may hold values from -6 to 6
- lengths: int32 [16], P('groups'), parts along dimension 0, may hold values from 192 to 768, as said below
- packing: int32 [16], P('groups'), parts along dimension 0, may hold values from 0 to 7, each once
- positions: int32 [16, 64], P('groups'), parts along dimension 0, may hold values from 0 to 767, as said below
- logged: int32 [16, 64], P('groups'), parts along dimension 0, may hold values from 0 to 16383
- w_uvqk: bfloat16 [1024, 1024], P(None, 'tensor'), may hold values from -0.1875 to 0.1875
- w_out: bfloat16 [256, 1024], P('tensor'), may hold values from -0.375 to 0.375
- catalogue: bfloat16 [16384, 1024], P(('item', 'dp', 'tensor')), may hold values from -0.46875 to 0.46875
Outputs:
- scoring_state: bfloat16 [1024, 1024], P(('groups', 'item', 'dp'), 'tensor'), parts along dimension 0
- log_propensity: float32 [1024], P(('groups', 'item', 'dp')), parts along dimension 0
There are 2 independent parts, one for each index of `groups`. A program takes and returns all parts, laid end to end along the dimension named above; an argument that names none is the same for every part. Nothing has to cross between parts.
Inputs may be any that keep to these rules, and one draw needn't show every extreme that they name: `lengths`: one history has exactly 768 valid events and one exactly 192. positions[h, k] < lengths[h]. `packing`: each history id appears once.
All inputs are finite; a program needn't handle non-finite values.
Results may differ from a plain program's by a relative error of at most 0.0048.
Values may be sent and summed in bfloat16 or wider, within the bound.
A program may use at most 64 MiB of HBM per device.

v0:
```python
import math
import jax
import jax.numpy as jnp
from jax import lax
from jax.sharding import PartitionSpec as P

DH = 128


def pick_target(logits, item_ids, item_base):
    local_ids = item_ids - item_base
    matches = jnp.arange(logits.shape[1], dtype=jnp.int32)[None, :] == local_ids[:, None]
    return jnp.sum(jnp.where(matches, logits, 0.0), axis=1)


def local(events, lengths, packing, positions, logged, w_uvqk, w_out, catalogue):
    slot_rows, model_width = events.shape
    hist_count = packing.shape[0]
    imp_count = positions.shape[1]
    local_heads = w_out.shape[0] // DH
    item_count = catalogue.shape[0]
    slot_index = lax.axis_index(("item", "dp"))
    hist_ids = jnp.arange(hist_count, dtype=jnp.int32)
    slot_pick = (packing[:, None] == hist_ids[None, :]).astype(jnp.int32)
    owned = (hist_ids == slot_index).astype(jnp.int32)
    hist_row = jnp.sum(slot_pick * owned[:, None], axis=0)
    hist_length = jnp.sum(hist_row * lengths)
    event_spots = jnp.sum(hist_row[:, None] * positions, axis=0)
    slot_items = jnp.sum(slot_pick[:, :, None] * logged[None, :, :], axis=1).reshape(
        hist_count * imp_count
    )
    item_base = lax.axis_index(("item", "dp", "tensor")) * item_count
    split_weights = w_uvqk.reshape(model_width, local_heads, 4, DH)
    w_values_keys = split_weights[:, :, 1::2].reshape(model_width, local_heads * 2 * DH)
    w_gate_query = split_weights[:, :, 0::2].reshape(model_width, local_heads * 2 * DH)
    values_keys = jnp.dot(events, w_values_keys, preferred_element_type=jnp.float32)
    values_keys = (
        jax.nn.silu(values_keys).astype(jnp.bfloat16).reshape(slot_rows, local_heads, 2, DH)
    )
    chosen = jnp.take(events, event_spots, axis=0)
    gate_query = jnp.dot(chosen, w_gate_query, preferred_element_type=jnp.float32)
    gate_query = jax.nn.silu(gate_query).astype(jnp.bfloat16).reshape(imp_count, local_heads, 2, DH)
    scores = jnp.einsum(
        "ied,med->iem",
        gate_query[:, :, 1],
        values_keys[:, :, 1],
        preferred_element_type=jnp.float32,
    ) / math.sqrt(DH)
    slot_range = jnp.arange(slot_rows, dtype=jnp.int32)
    is_valid = (slot_range[None, :] <= event_spots[:, None]) & (slot_range[None, :] < hist_length)
    weights = jnp.where(is_valid[:, None, :], jax.nn.silu(scores), 0.0).astype(jnp.bfloat16)
    attended = jnp.einsum(
        "iem,med->ied", weights, values_keys[:, :, 0], preferred_element_type=jnp.float32
    )
    inverse = lax.rsqrt(jnp.mean(attended * attended, axis=-1, keepdims=True) + 1e-06)
    gated_rows = (attended * inverse * gate_query[:, :, 0].astype(jnp.float32)).astype(jnp.bfloat16)
    gated_rows = gated_rows.reshape(imp_count, local_heads * DH)
    partial_out = jnp.dot(gated_rows, w_out, preferred_element_type=jnp.float32)
    residual = chosen.astype(jnp.float32)
    col_share = model_width // lax.axis_size("tensor")
    col_start = lax.axis_index("tensor") * col_share
    summed = lax.psum(partial_out, "tensor")
    hidden_state = (summed + residual).astype(jnp.bfloat16)
    state_out = lax.dynamic_slice_in_dim(hidden_state, col_start, col_share, 1)
    logits = lax.dot_general(
        lax.all_gather(hidden_state, ("item", "dp"), axis=0, tiled=True),
        catalogue,
        (((1,), (1,)), ((), ())),
        preferred_element_type=jnp.float32,
    )
    new_totals = jnp.sum(jnp.exp(logits), axis=1)
    new_target = pick_target(logits, slot_items, item_base)
    whole_totals, whole_target = lax.psum((new_totals, new_target), ("item", "dp", "tensor"))
    mine_totals = lax.dynamic_slice_in_dim(whole_totals, slot_index * imp_count, imp_count, 0)
    mine_target = lax.dynamic_slice_in_dim(whole_target, slot_index * imp_count, imp_count, 0)
    return (state_out, mine_target - jnp.log(mine_totals))


def solution(mesh):
    placed = (
        P(("groups", "item", "dp"), None),
        P("groups"),
        P("groups"),
        P("groups", None),
        P("groups", None),
        P(None, "tensor"),
        P("tensor", None),
        P(("item", "dp", "tensor"), None),
    )
    return jax.shard_map(
        local,
        mesh=mesh,
        in_specs=placed,
        out_specs=(P(("groups", "item", "dp"), "tensor"), P(("groups", "item", "dp"))),
        check_vma=False,
    )
```

profile of v0, /device:TPU:0, one launch (start us, length us, event | category | flops | bytes accessed | tf_op | source)
XLA Modules:
  0.0 136.1 jit_solution(11309855949234600494)
XLA Ops:
  7.2 0.0 copy-start
  7.2 0.0 all-reduce.3.cloned.1.call-start
  7.2 0.9 select_reduce_fusion.1
  8.1 0.8 multiply_reduce_fusion.2
  8.9 1.3 reshape.175
  10.3 0.0 copy-start.5
  10.3 12.4 %slice.21 = bf16[1024,1,2,128]{3,2,0,1:T(2,128)(2,1)} slice(bf16[1024,1,4,128]{3,2,0,1:T(4,128)(2,1)S(1)} %reshape.175), slice={[0:1024:1], [0:1:1], [0:4:2], [0:128:1]} | slice | bytes 1048576 | tf_op jit(solution)/shard_map/slice | solution.py:35
  22.6 12.4 %slice.18 = bf16[1024,1,2,128]{3,2,0,1:T(2,128)(2,1)} slice(bf16[1024,1,4,128]{3,2,0,1:T(4,128)(2,1)S(1)} %reshape.175), slice={[0:1024:1], [0:1:1], [1:4:2], [0:128:1]} | slice | bytes 1048576 | tf_op jit(solution)/shard_map/slice | solution.py:34
  35.0 0.0 copy-start.1
  35.0 2.5 %gather_fusion = bf16[64,1024]{1,0:T(8,128)(2,1)S(1)} fusion(bf16[768,1024]{1,0:T(8,128)(2,1)} %param.8, s32[1024]{0:T(1024)S(1)} %pad_clamp_fusion), kind=kCustom, calls=%fused_computation | custom fusion | bytes 262400 | tf_op jit(solution)/shard_map/jit(_take)/gather | solution.py:40
  37.5 1.3 multiply_convert_fusion.1
  38.8 0.1 fusion.30
  38.9 0.0 copy-done.5
  38.9 0.6 multiply_reduce_fusion.3
  39.5 0.6 iota_compare_fusion.2
  40.2 0.0 copy-done.1
  40.2 0.0 copy-start.2
  40.2 2.1 %multiply_convert_fusion = bf16[768,256]{0,1:T(8,128)(2,1)S(1)} fusion(bf16[768,1024]{1,0:T(8,128)(2,1)} %param.8, bf16[128,8,2,128]{3,2,1,0:T(2,128)(2,1)S(1)} %bitcast.81), kind=kOutput, calls=%fused_computation.7 | convolution fusion | flops 403636224 | bytes 2490368 | tf_op jit(solution)/shard_map/dot_general | solution.py:36
  42.4 0.0 copy-start.4
  42.4 0.0 copy-start.3
  42.4 0.4 multiply_reduce_fusion.1
  42.8 0.0 copy-done.2
  42.8 0.9 fusion.21
  43.8 0.0 all-reduce.3.cloned.1.call-update
  43.8 0.0 all-gather.2.cloned.1.call-start
  43.9 26.0 %all-reduce.3.cloned.1.call-done = f32[64,1024]{1,0:T(8,128)} async-done(((f32[64,1024]{1,0:T(8,128)}), f32[64,1024]{1,0:T(8,128)}) %all-reduce.3.cloned.1.call-update) | async-done | bytes 262160 | tf_op jit(solution)/shard_map/psum | solution.py:62
  69.8 1.7 %add_convert_fusion = bf16[64,1024]{1,0:T(8,128)(2,1)} fusion(f32[64,1024]{1,0:T(8,128)} %all-reduce.3.cloned.1.call-done, bf16[64,1024]{1,0:T(8,128)(2,1)S(1)} %gather_fusion, pred[64]{0:T(512)(128)(4,1)S(1)} %compare_and_fusion), kind=kLoop, calls=%fused_computation.14 | loop fusion | flops 262144 | bytes 524352 | tf_op jit(solution)/shard_map/convert_element_type | solution.py:63
  71.5 0.0 all-gather.2.cloned.1.call-update
  71.6 0.0 copy-done.4
  71.6 0.1 fusion.24
  71.6 0.0 copy-done.3
  71.7 0.1 multiply_reduce_fusion
  71.8 0.1 sub.18
  71.8 1.5 %constant_dynamic-slice_fusion = bf16[64,512]{1,0:T(8,128)(2,1)} fusion(bf16[64,1024]{1,0:T(8,128)(2,1)} %add_convert_fusion, s32[]{:T(128)S(6)} %select_n.39), kind=kLoop, calls=%fused_computation.52 | loop fusion | bytes 131076 | tf_op jit(solution)/shard_map/dynamic_slice | solution.py:64
  73.3 20.5 %all-gather.2.cloned.1.call-done = bf16[512,1024]{1,0:T(8,128)(2,1)} async-done(((bf16[64,1024]{1,0:T(8,128)(2,1)}), bf16[512,1024]{1,0:T(8,128)(2,1)}) %all-gather.2.cloned.1.call-update) | async-done | bytes 1048592 | tf_op jit(solution)/shard_map/all_gather | solution.py:66
  93.8 0.0 copy-done
  93.8 2.8 %select_reduce_fusion = (f32[512]{0:T(512)S(1)}, f32[512]{0:T(512)S(1)}) fusion(s32[512]{0:T(512)S(1)} %sub.18, bf16[512,1024]{1,0:T(8,128)(2,1)} %all-gather.2.cloned.1.call-done, bf16[1024,1024]{1,0:T(8,128)(2,1)S(1)} %copy-done), kind=kOutput, calls=%fused_computation.2 | convolution fusion | flops 1075837952 | bytes 3151872 | tf_op jit(solution)/shard_map/dot_general | solution.py:65
  96.6 32.1 %all-reduce = (f32[512]{0:T(512)S(1)}, f32[512]{0:T(512)S(1)}) all-reduce(f32[512]{0:T(512)S(1)} %get-tuple-element.3, f32[512]{0:T(512)S(1)} %get-tuple-element.2), channel_id=1, replica_groups=mesh['groups'=2,'item'=4,'dp'=2,'tensor'=2] {'item','dp','tensor'}, use_global_device_ids=true, to_apply=%region_9.10 | all-reduce | flops 1024 | bytes 8192 | tf_op jit(solution)/shard_map/psum | solution.py:73
  128.7 0.6 log_subtract_fusion
  (7 shorter events, 0.1 us)
Async XLA Ops:
  7.2 86.7 %copy-start = (bf16[1024,1024]{1,0:T(8,128)(2,1)S(1)}, bf16[1024,1024]{1,0:T(8,128)(2,1)}, u32[]{:S(2)}) copy-start(bf16[1024,1024]{1,0:T(8,128)(2,1)} %param.15) | copy-start | bytes 6291460
  7.2 62.7 %all-reduce.3.cloned.1.call-start = ((), (), s32[]{:S(2)}) async-start(), calls=%async_computation | async-start | bytes 524288 | tf_op jit(solution)/shard_map/psum | solution.py:62
  10.3 28.6 %copy-start.5 = (s32[8]{0:T(128)S(1)}, s32[8]{0:T(128)}, u32[]{:S(2)}) copy-start(s32[8]{0:T(128)} %param.9) | copy-start | bytes 100
  35.0 5.2 %copy-start.1 = (bf16[1024,1,2,128]{3,2,0,1:T(2,128)(2,1)S(1)}, bf16[1024,1,2,128]{3,2,0,1:T(2,128)(2,1)}, u32[]{:S(2)}) copy-start(bf16[1024,1,2,128]{3,2,0,1:T(2,128)(2,1)} %slice.18) | copy-start | bytes 1572868
  40.2 2.6 %copy-start.2 = (bf16[128,1024]{1,0:T(8,128)(2,1)S(1)}, bf16[128,1024]{1,0:T(8,128)(2,1)}, u32[]{:S(2)}) copy-start(bf16[128,1024]{1,0:T(8,128)(2,1)} %param.14) | copy-start | bytes 786436
  42.4 29.2 %copy-start.4 = (s32[8]{0:T(128)S(1)}, s32[8]{0:T(128)}, u32[]{:S(2)}) copy-start(s32[8]{0:T(128)} %param.10) | copy-start | bytes 100
  42.4 29.3 %copy-start.3 = (s32[8,64]{1,0:T(8,128)S(1)}, s32[8,64]{1,0:T(8,128)}, u32[]{:S(2)}) copy-start(s32[8,64]{1,0:T(8,128)} %param.12) | copy-start | bytes 6148
  43.8 50.0 %all-gather.2.cloned.1.call-start = ((), (), s32[]{:S(2)}) async-start(), calls=%async_computation.1 | async-start | bytes 1179648 | tf_op jit(solution)/shard_map/all_gather | solution.py:66
Sparse Core Ops, SparseCore 0:
  43.9 25.8 all-reduce.2
  71.7 22.0 all-gather.1
where the time goes:
time: 137 us; the launch traced here: 136 us
  waiting for transfers between devices  46.5 us (34%)
  blocking collectives  32.1 us (23%)
  local copies, waits for them, and re-layouts  30.2 us (22%)
  between operations  14.2 us (10%)
  matrix products  7.63 us (6%)
  other arithmetic  5.41 us (4%)
    psum x1, blocking collectives, local(): lax.psum((new_totals, new_target), ('item', 'dp', 'tensor'))  32.1 us
    psum x1, waiting for transfers between devices, local(): summed = lax.psum(partial_out, 'tensor')  26 us
    all_gather x1, waiting for transfers between devices, local(): lax.all_gather(hidden_state, ('item', 'dp'), axis=0, tiled=True)  20.5 us
    slice x1, local copies, waits for them, and re-layouts, local(): split_weights[:, :, 1::2].reshape(model_width, local_heads * 2 * DH)  12.4 us
    slice x1, local copies, waits for them, and re-layouts, local(): split_weights[:, :, 0::2].reshape(model_width, local_heads * 2 * DH)  12.4 us
    dot_general x1, matrix products, local(): lax.dot_general(lax.all_gather(hidden_state, ('item', 'dp'), axis=0, tile...  2.82 us
  transfers between devices with their start and end apart: 2, of which 2 were waited for; matrix products, arithmetic and copies ran while one was open for 1% of the time, Pallas kernels for 0%

commit v1 on v0

--- a/solution.py
+++ b/solution.py
@@ -70,7 +70,9 @@
     )
     new_totals = jnp.sum(jnp.exp(logits), axis=1)
     new_target = pick_target(logits, slot_items, item_base)
-    whole_totals, whole_target = lax.psum((new_totals, new_target), ("item", "dp", "tensor"))
+    whole_totals, whole_target = lax.psum(
+        lax.psum((new_totals, new_target), ("dp", "tensor")), "item"
+    )
     mine_totals = lax.dynamic_slice_in_dim(whole_totals, slot_index * imp_count, imp_count, 0)
     mine_target = lax.dynamic_slice_in_dim(whole_target, slot_index * imp_count, imp_count, 0)
     return (state_out, mine_target - jnp.log(mine_totals))

time: 137 us -> 122 us (0.89)
  blocking collectives: 32.1 us -> 17.7 us
    psum x1 -> x2, blocking collectives: 32.1 us -> 17.7 us  [the longest x1 10.2 us: local(): lax.psum(lax.psum((new_totals, new_target), ('dp', 'tensor')), 'item')]
where the time goes in v1:
time: 122 us
  waiting for transfers between devices  46.5 us (38%)
  local copies, waits for them, and re-layouts  30.2 us (25%)
  blocking collectives  17.7 us (15%)
  between operations  14.2 us (12%)
  matrix products  7.63 us (6%)
  other arithmetic  5.41 us (4%)
    psum x1, waiting for transfers between devices, local(): summed = lax.psum(partial_out, 'tensor')  26 us
    all_gather x1, waiting for transfers between devices, local(): lax.all_gather(hidden_state, ('item', 'dp'), axis=0, tiled=True)  20.5 us
    slice x1, local copies, waits for them, and re-layouts, local(): split_weights[:, :, 1::2].reshape(model_width, local_heads * 2 * DH)  12.4 us
    slice x1, local copies, waits for them, and re-layouts, local(): split_weights[:, :, 0::2].reshape(model_width, local_heads * 2 * DH)  12.4 us
    psum x1, blocking collectives, local(): lax.psum(lax.psum((new_totals, new_target), ('dp', 'tensor')), 'item')  10.2 us
    psum x1, blocking collectives, local(): lax.psum((new_totals, new_target), ('dp', 'tensor'))  7.44 us
    dot_general x1, matrix products, local(): lax.dot_general(lax.all_gather(hidden_state, ('item', 'dp'), axis=0, tile...  2.82 us
    gather x1, local copies, waits for them, and re-layouts, local(): chosen = jnp.take(events, event_spots, axis=0)  2.47 us
  transfers between devices with their start and end apart: 2, of which 2 were waited for; matrix products, arithmetic and copies ran while one was open for 1% of the time, Pallas kernels for 0%

profile of v1, /device:TPU:0, one launch (start us, length us, event | category | flops | bytes accessed | tf_op | source)
XLA Modules:
  0.0 121.7 jit_solution(14283400310211065381)
XLA Ops:
  7.2 0.0 copy-start
  7.2 0.0 all-reduce.4.cloned.1.call-start
  7.2 0.9 select_reduce_fusion.1
  8.1 0.8 multiply_reduce_fusion.2
  8.9 1.3 %reshape.175 = bf16[1024,1,4,128]{3,2,0,1:T(4,128)(2,1)S(1)} reshape(bf16[1024,512]{1,0:T(8,128)(2,1)} %param.13) | data formatting | bytes 2097152 | tf_op jit(solution)/shard_map/reshape | solution.py:33
  10.3 0.0 copy-start.5
  10.3 12.4 %slice.21 = bf16[1024,1,2,128]{3,2,0,1:T(2,128)(2,1)} slice(bf16[1024,1,4,128]{3,2,0,1:T(4,128)(2,1)S(1)} %reshape.175), slice={[0:1024:1], [0:1:1], [0:4:2], [0:128:1]} | slice | bytes 1048576 | tf_op jit(solution)/shard_map/slice | solution.py:35
  22.6 12.4 %slice.18 = bf16[1024,1,2,128]{3,2,0,1:T(2,128)(2,1)} slice(bf16[1024,1,4,128]{3,2,0,1:T(4,128)(2,1)S(1)} %reshape.175), slice={[0:1024:1], [0:1:1], [1:4:2], [0:128:1]} | slice | bytes 1048576 | tf_op jit(solution)/shard_map/slice | solution.py:34
  35.0 0.0 copy-start.1
  35.0 2.5 %gather_fusion = bf16[64,1024]{1,0:T(8,128)(2,1)S(1)} fusion(bf16[768,1024]{1,0:T(8,128)(2,1)} %param.8, s32[1024]{0:T(1024)S(1)} %pad_clamp_fusion), kind=kCustom, calls=%fused_computation | custom fusion | bytes 262400 | tf_op jit(solution)/shard_map/jit(_take)/gather | solution.py:40
  37.5 1.3 %multiply_convert_fusion.1 = bf16[64,256]{1,0:T(8,128)(2,1)S(1)} fusion(bf16[128,8,2,128]{3,2,1,0:T(2,128)(2,1)} %bitcast.82, bf16[64,1024]{1,0:T(8,128)(2,1)S(1)} %gather_fusion, pred[64]{0:T(512)(128)(4,1)S(1)} %compare_and_fusion), kind=kOutput, calls=%fused_computation.27 | convolution fusion | flops 33701888 | bytes 688192 | tf_op jit(solution)/shard_map/dot_general | solution.py:41
  38.8 0.1 fusion.30
  38.9 0.0 copy-done.5
  38.9 0.6 multiply_reduce_fusion.3
  39.5 0.6 iota_compare_fusion.2
  40.2 0.0 copy-done.1
  40.2 0.0 copy-start.2
  40.2 2.1 %multiply_convert_fusion = bf16[768,256]{0,1:T(8,128)(2,1)S(1)} fusion(bf16[768,1024]{1,0:T(8,128)(2,1)} %param.8, bf16[128,8,2,128]{3,2,1,0:T(2,128)(2,1)S(1)} %bitcast.81), kind=kOutput, calls=%fused_computation.7 | convolution fusion | flops 403636224 | bytes 2490368 | tf_op jit(solution)/shard_map/dot_general | solution.py:36
  42.4 0.0 copy-start.4
  42.4 0.0 copy-start.3
  42.4 0.4 multiply_reduce_fusion.1
  42.8 0.0 copy-done.2
  42.8 0.9 fusion.21
  43.8 0.0 all-reduce.4.cloned.1.call-update
  43.8 0.0 all-gather.2.cloned.1.call-start
  43.9 26.0 %all-reduce.4.cloned.1.call-done = f32[64,1024]{1,0:T(8,128)} async-done(((f32[64,1024]{1,0:T(8,128)}), f32[64,1024]{1,0:T(8,128)}) %all-reduce.4.cloned.1.call-update) | async-done | bytes 262160 | tf_op jit(solution)/shard_map/psum | solution.py:62
  69.8 1.7 %add_convert_fusion = bf16[64,1024]{1,0:T(8,128)(2,1)} fusion(f32[64,1024]{1,0:T(8,128)} %all-reduce.4.cloned.1.call-done, bf16[64,1024]{1,0:T(8,128)(2,1)S(1)} %gather_fusion, pred[64]{0:T(512)(128)(4,1)S(1)} %compare_and_fusion), kind=kLoop, calls=%fused_computation.14 | loop fusion | flops 262144 | bytes 524352 | tf_op jit(solution)/shard_map/convert_element_type | solution.py:63
  71.5 0.0 all-gather.2.cloned.1.call-update
  71.6 0.0 copy-done.4
  71.6 0.1 fusion.24
  71.6 0.0 copy-done.3
  71.7 0.1 multiply_reduce_fusion
  71.8 0.1 sub.18
  71.8 1.5 %constant_dynamic-slice_fusion = bf16[64,512]{1,0:T(8,128)(2,1)} fusion(bf16[64,1024]{1,0:T(8,128)(2,1)} %add_convert_fusion, s32[]{:T(128)S(6)} %select_n.39), kind=kLoop, calls=%fused_computation.52 | loop fusion | bytes 131076 | tf_op jit(solution)/shard_map/dynamic_slice | solution.py:64
  73.3 20.5 %all-gather.2.cloned.1.call-done = bf16[512,1024]{1,0:T(8,128)(2,1)} async-done(((bf16[64,1024]{1,0:T(8,128)(2,1)}), bf16[512,1024]{1,0:T(8,128)(2,1)}) %all-gather.2.cloned.1.call-update) | async-done | bytes 1048592 | tf_op jit(solution)/shard_map/all_gather | solution.py:66
  93.8 0.0 copy-done
  93.8 2.8 %select_reduce_fusion = (f32[512]{0:T(512)S(1)}, f32[512]{0:T(512)S(1)}) fusion(s32[512]{0:T(512)S(1)} %sub.18, bf16[512,1024]{1,0:T(8,128)(2,1)} %all-gather.2.cloned.1.call-done, bf16[1024,1024]{1,0:T(8,128)(2,1)S(1)} %copy-done), kind=kOutput, calls=%fused_computation.2 | convolution fusion | flops 1075837952 | bytes 3151872 | tf_op jit(solution)/shard_map/dot_general | solution.py:65
  96.6 7.4 %all-reduce = (f32[512]{0:T(512)S(1)}, f32[512]{0:T(512)S(1)}) all-reduce(f32[512]{0:T(512)S(1)} %get-tuple-element.3, f32[512]{0:T(512)S(1)} %get-tuple-element.2), channel_id=1, replica_groups=mesh['groups'=2,'item'=4,'dp'=2,'tensor'=2] {'dp','tensor'}, use_global_device_ids=true, to_apply=%region_10.11 | all-reduce | flops 1024 | bytes 8192 | tf_op jit(solution)/shard_map/psum | solution.py:74
  104.1 10.2 %all-reduce.1 = (f32[512]{0:T(512)S(1)}, f32[512]{0:T(512)S(1)}) all-reduce(f32[512]{0:T(512)S(1)} %get-tuple-element.4, f32[512]{0:T(512)S(1)} %get-tuple-element.5), channel_id=1, replica_groups=mesh['groups'=2,'item'=4,'dp'=2,'tensor'=2] {'item'}, use_global_device_ids=true, to_apply=%region_11.12 | all-reduce | flops 1024 | bytes 8192 | tf_op jit(solution)/shard_map/psum | solution.py:73
  114.3 0.6 log_subtract_fusion
  (7 shorter events, 0.1 us)
Async XLA Ops:
  7.2 86.7 %copy-start = (bf16[1024,1024]{1,0:T(8,128)(2,1)S(1)}, bf16[1024,1024]{1,0:T(8,128)(2,1)}, u32[]{:S(2)}) copy-start(bf16[1024,1024]{1,0:T(8,128)(2,1)} %param.15) | copy-start | bytes 6291460
  7.2 62.7 %all-reduce.4.cloned.1.call-start = ((), (), s32[]{:S(2)}) async-start(), calls=%async_computation | async-start | bytes 524288 | tf_op jit(solution)/shard_map/psum | solution.py:62
  10.3 28.6 %copy-start.5 = (s32[8]{0:T(128)S(1)}, s32[8]{0:T(128)}, u32[]{:S(2)}) copy-start(s32[8]{0:T(128)} %param.9) | copy-start | bytes 100
  35.0 5.2 %copy-start.1 = (bf16[1024,1,2,128]{3,2,0,1:T(2,128)(2,1)S(1)}, bf16[1024,1,2,128]{3,2,0,1:T(2,128)(2,1)}, u32[]{:S(2)}) copy-start(bf16[1024,1,2,128]{3,2,0,1:T(2,128)(2,1)} %slice.18) | copy-start | bytes 1572868
  40.2 2.6 %copy-start.2 = (bf16[128,1024]{1,0:T(8,128)(2,1)S(1)}, bf16[128,1024]{1,0:T(8,128)(2,1)}, u32[]{:S(2)}) copy-start(bf16[128,1024]{1,0:T(8,128)(2,1)} %param.14) | copy-start | bytes 786436
  42.4 29.2 %copy-start.4 = (s32[8]{0:T(128)S(1)}, s32[8]{0:T(128)}, u32[]{:S(2)}) copy-start(s32[8]{0:T(128)} %param.10) | copy-start | bytes 100
  42.4 29.3 %copy-start.3 = (s32[8,64]{1,0:T(8,128)S(1)}, s32[8,64]{1,0:T(8,128)}, u32[]{:S(2)}) copy-start(s32[8,64]{1,0:T(8,128)} %param.12) | copy-start | bytes 6148
  43.8 50.0 %all-gather.2.cloned.1.call-start = ((), (), s32[]{:S(2)}) async-start(), calls=%async_computation.1 | async-start | bytes 1179648 | tf_op jit(solution)/shard_map/all_gather | solution.py:66
Sparse Core Ops, SparseCore 0:
  43.9 25.8 all-reduce.3
  71.7 22.0 all-gather.1
